TPU v7x, 128 devices: a whole 4x4x4 slice. The times are simulated.
128 devices in a mesh: tm: 4 (over z_lo, core), freq: 32 (over y, z_hi, x).
Axes of the slice: x: 4, y: 4, z: 4 (z_hi: 2, z_lo: 2; z = z_hi * 2 + z_lo), core: 2. Of those that a mesh axis runs over, the one named last changes fastest.
Arguments:
- voltages: bfloat16 [4, 1024, 258048], P('tm', 'freq'), may hold values from -6 to 6
- chan_bins: int32 [128], replicated, may hold values from 0 to 2047, as said below
- antenna_map: int32 [1024], replicated, may hold values from 0 to 1023, each once
- beam_index: int32 [512], replicated, may hold values from 0 to 511, each once
- delays: float32 [512, 1024], replicated, may hold values from -4 to 4
Outputs:
- visibilities: float32 [128, 2, 1024, 1024], P(('tm', 'freq'))
- beam_volts: float32 [512, 128, 2, 192], P('freq', 'tm')
Inputs may be any that keep to these rules, and one draw needn't show every extreme that they name: `chan_bins`: the 128 bins are distinct, below 2048. `antenna_map`: each signal feeds exactly one antenna input. `beam_index`: each beam has a pointing of its own.
All inputs are finite; a program needn't handle non-finite values.
Results may differ from a plain program's by a relative error of at most 0.006.
Values may be sent and summed in bfloat16 or wider, within the bound.
A program may use at most 128 MiB of HBM per device.

v0:
```python
import math

import jax
import jax.numpy as jnp
from jax import lax
from jax.sharding import PartitionSpec as P

NFFT = 4096
TAPS = 16


def prototype(tap_count, length):
    total = tap_count * length
    offsets = jnp.arange(total, dtype=jnp.float32)
    shifted = (offsets - 0.5 * total + 0.5) / length
    window = 0.5 - 0.5 * jnp.cos(2.0 * math.pi / total * (offsets + 0.5))
    return (jnp.sinc(shifted) * window).reshape(tap_count, length)


def dft_table(bins, length):
    positions = jnp.arange(length, dtype=jnp.int32)
    products = bins[:, None] * positions[None, :] % length
    angles = products.astype(jnp.float32) * (2.0 * math.pi / length)
    scale = 1.0 / math.sqrt(length)
    return jnp.stack([jnp.cos(angles) * scale, -jnp.sin(angles) * scale]).astype(jnp.bfloat16)


def filter_bank(samples, taps_table, frames):
    total = jnp.zeros((samples.shape[0], frames, samples.shape[2]), jnp.float32)
    for tap_index in range(taps_table.shape[0]):
        total = total + taps_table[tap_index] * samples[
            :, tap_index : tap_index + frames, :
        ].astype(jnp.float32)
    return total.astype(jnp.bfloat16)


def body(voltages, chan_bins, antenna_map, beam_index, delays):
    signals_dev = voltages.shape[1]
    frames = voltages.shape[2] // NFFT - TAPS + 1
    channels = chan_bins.shape[0]
    tm_count = lax.axis_size("tm")
    freq_count = lax.axis_size("freq")
    taps_table = prototype(TAPS, NFFT)
    table = dft_table(chan_bins, NFFT)
    samples = voltages[0].reshape(signals_dev, frames + TAPS - 1, NFFT)
    filtered = filter_bank(samples, taps_table, frames).reshape(signals_dev * frames, NFFT)
    spectra = jnp.einsum("rcn,mn->crm", table, filtered, preferred_element_type=jnp.float32)
    spectra = spectra.astype(jnp.bfloat16).reshape(channels, 2, signals_dev, frames)
    moved = lax.all_to_all(
        spectra[:, :, None], ("tm", "freq"), split_axis=0, concat_axis=2, tiled=True
    )
    moved = moved.reshape(2, tm_count, freq_count, signals_dev, frames).transpose(0, 2, 3, 1, 4)
    moved = moved.reshape(2, freq_count * signals_dev, tm_count * frames)
    volts = jnp.take(moved, antenna_map, axis=1)
    swapped = jnp.stack([volts[1], -volts[0]])
    real_part = jnp.einsum("rat,rbt->ab", volts, volts, preferred_element_type=jnp.float32)
    imag_part = jnp.einsum("rat,rbt->ab", swapped, volts, preferred_element_type=jnp.float32)
    visibilities = jnp.stack([real_part, imag_part]) / volts.shape[2]
    channel = lax.axis_index("tm") * freq_count + lax.axis_index("freq")
    bin_value = lax.dynamic_index_in_dim(chan_bins, channel, keepdims=False)
    selected = jnp.take(delays, beam_index, axis=0)
    phase = selected * bin_value.astype(jnp.float32) * (2.0 * math.pi / NFFT)
    cosine = jnp.cos(phase).astype(jnp.bfloat16)
    sine = jnp.sin(phase).astype(jnp.bfloat16)
    weights = jnp.stack([jnp.stack([cosine, sine], 1), jnp.stack([-sine, cosine], 1)])
    formed = jnp.einsum("obra,rat->bot", weights, volts, preferred_element_type=jnp.float32)
    formed = formed * (1.0 / math.sqrt(volts.shape[1]))
    turned = lax.all_to_all(formed[:, None], "freq", split_axis=0, concat_axis=1, tiled=True)
    return (visibilities[None], turned)


def solution(mesh):
    return jax.shard_map(
        body,
        mesh=mesh,
        in_specs=(P("tm", "freq", None), P(), P(), P(), P()),
        out_specs=(P(("tm", "freq"), None, None, None), P("freq", "tm", None, None)),
        check_vma=False,
    )
```

profile of v0, /device:TPU:0, one launch (start us, length us, event | category | flops | bytes accessed | tf_op | source)
XLA Modules:
  0.0 247.3 jit_solution(6298408112098288089)
XLA Ops:
  0.6 0.0 copy-start
  0.6 1.2 fusion.34
  1.9 0.0 copy-start.4
  1.9 15.8 %reshape_squeeze.3 = bf16[32,63,4096]{2,1,0:T(8,128)(2,1)} reshape(bf16[1,32,258048]{2,1,0:T(8,128)(2,1)} %param.5) | data formatting | bytes 33030144 | tf_op jit(solution)/shard_map/reshape;squeeze | solution.py:45
  17.8 0.0 copy-done.4
  17.8 9.0 %multiply_convert_fusion.1 = (bf16[1,128,4096]{2,1,0:T(8,128)(2,1)S(1)}, bf16[1,128,4096]{2,1,0:T(8,128)(2,1)S(1)}) fusion(s32[128]{0:T(128)S(1)} %copy-done.4), kind=kLoop, calls=%fused_computation.28 | loop fusion | flops 9961472 | bytes 2097664 | tf_op jit(solution)/shard_map/convert
  26.8 108.6 %add_convert_fusion = bf16[32,48,4096]{2,1,0:T(8,128)(2,1)} fusion(bf16[32,63,4096]{2,1,0:T(8,128)(2,1)} %reshape_squeeze.3, f32[4096]{0:T(1024)S(1)} %get-tuple-element.13, f32[4096]{0:T(1024)S(1)} %get-tuple-element.14, f32[4096]{0:T(1024)S(1)} %get-tuple-element.15, f32[4096]{0:T(1024)S(1)} %get-tuple-element.16, f32[4096]{0:T(1024)S(1)} %get-tuple-element.17, ...), kind=kLoop, calls=%fused_computation.2 | loop fusion | flops 301989888 | bytes 214171648 | tf_op jit(solution)/shard_map/convert_element_type | solution.py:34
  135.4 0.0 copy-start.3
  135.4 6.8 %convolution_convert_fusion = bf16[1536,2,128]{2,0,1:T(8,128)(2,1)S(1)} fusion(bf16[1536,4096,1]{1,0,2:T(8,128)(2,1)} %bitcast.65, bf16[1,128,4096]{2,1,0:T(8,128)(2,1)S(1)} %get-tuple-element.29, bf16[1,128,4096]{2,1,0:T(8,128)(2,1)S(1)} %get-tuple-element.28), kind=kOutput, calls=%fused_computation.11 | convolution fusion | flops 3225812992 | bytes 15466496 | tf_op jit(solution)/shard_map/rcn,mn->crm/dot_general | solution.py:47
  142.2 3.7 %copy.14 = bf16[128,2,1,32,48]{4,3,1,2,0:T(8,128)(2,1)} copy(bf16[128,2,1,32,48]{0,4,3,1,2:T(8,128)(2,1)S(1)} %bitcast.69) | data formatting | bytes 1572864 | tf_op jit(solution)/shard_map/broadcast_in_dim;reshape | solution.py:50
  145.9 5.9 %reshape.319 = bf16[128,2,1536]{2,1,0:T(2,128)(2,1)} reshape(bf16[128,1,2,32,48]{4,3,2,1,0:T(8,128)(2,1)} %bitcast.66) | data formatting | bytes 1572864
  151.8 11.4 %all-to-all-start = ((bf16[128,2,1536]{2,1,0:T(2,128)(2,1)}), bf16[128,2,1536]{2,1,0:T(2,128)(2,1)S(1)}, u32[]{:S(2)}, u32[]{:S(2)}) async-start(bf16[128,2,1536]{2,1,0:T(2,128)(2,1)} %reshape.319), calls=%async_computation | async-start | bytes 1572864 | tf_op jit(solution)/shard_map/all_to_all | solution.py:49
  163.2 0.0 copy-done.3
  163.3 0.6 dynamic_slice.4
  164.5 0.0 copy-done
  164.5 2.7 %gather_fusion.1 = f32[512,1024]{1,0:T(8,128)} fusion(f32[512,1024]{1,0:T(8,128)S(1)} %copy-done, s32[1024]{0:T(1024)S(1)} %pad_clamp_fusion), kind=kCustom, calls=%fused_computation.1 | custom fusion | bytes 4196352 | tf_op jit(solution)/shard_map/jit(_take)/gather | solution.py:61
  167.2 0.0 copy-start.2
  167.2 8.8 %fusion.64 = (bf16[512,1,1024]{2,0,1:T(8,128)(2,1)S(1)}, bf16[512,1,1024]{2,0,1:T(8,128)(2,1)S(1)}) fusion(f32[]{:T(128)} %bitcast.16, f32[512,1024]{1,0:T(8,128)} %gather_fusion.1, pred[512]{0:T(512)(128)(4,1)S(1)} %compare_and_fusion.1), kind=kLoop, calls=%fused_computation.90 | loop fusion | flops 3670016 | bytes 4194820 | tf_op jit(solution)/shard_map/neg | solution.py:65
  176.0 8.5 %cosine_convert_fusion = bf16[512,1,1024]{2,0,1:T(8,128)(2,1)S(1)} fusion(f32[512,1024]{1,0:T(8,128)} %gather_fusion.1, f32[]{:T(128)} %bitcast.16, pred[512]{0:T(512)(128)(4,1)S(1)} %compare_and_fusion.1), kind=kLoop, calls=%fused_computation.26 | loop fusion | flops 2097152 | bytes 3146244 | tf_op jit(solution)/shard_map/convert_element_type | solution.py:63
  184.5 2.3 maximum_bitcast_fusion
  186.8 0.0 copy-done.2
  186.9 0.0 all-to-all-done
  186.9 3.1 %reshape.320 = bf16[128,1,2,32,48]{4,3,2,1,0:T(8,128)(2,1)} reshape(bf16[128,2,1536]{2,1,0:T(2,128)(2,1)S(1)} %all-to-all-done) | data formatting | bytes 1572864
  189.9 4.9 %copy.24 = bf16[2,32,32,4,48]{4,3,0,2,1:T(4,128)(2,1)} copy(bf16[2,32,32,4,48]{4,2,0,1,3:T(8,128)(2,1)} %bitcast.67) | data formatting | bytes 1572864 | tf_op jit(solution)/shard_map/reshape | solution.py:53
  194.8 4.3 %reshape.318 = bf16[2,1024,192]{2,0,1:T(2,128)(2,1)S(1)} reshape(bf16[2,32,32,4,48]{4,3,0,2,1:T(4,128)(2,1)} %copy.24) | data formatting | bytes 1572864 | tf_op jit(solution)/shard_map/reshape | solution.py:53
  199.2 8.5 %gather_fusion = bf16[1024,2,192]{2,1,0:T(2,128)(2,1)} fusion(bf16[2,1024,192]{2,0,1:T(2,128)(2,1)S(1)} %reshape.318, s32[1024]{0:T(1024)S(1)} %fusion.59), kind=kCustom, calls=%fused_computation | custom fusion | bytes 1576960 | tf_op jit(solution)/shard_map/jit(_take)/gather | solution.py:54
  207.7 2.4 copy.18
  210.1 1.0 fusion.28
  211.0 4.6 %fusion.21 = f32[512,1,2,192]{0,3,2,1:T(8,128)} fusion(bf16[1,512,2,1024]{3,1,2,0:T(8,128)(2,1)} %get-tuple-element.9, bf16[1,512,2,1024]{3,1,2,0:T(8,128)(2,1)} %get-tuple-element.8, bf16[1024,2,192]{0,2,1:T(8,128)(2,1)S(1)} %copy.18, pred[1024]{0:T(1024)(128)(4,1)S(1)} %compare_and_fusion), kind=kOutput, calls=%fused_computation.34 | convolution fusion | flops 814284800 | bytes 5768192 | tf_op jit(solution)/shard_map/obra,rat->bot/dot_general | solution.py:66
  215.7 2.2 copy.19
  217.9 9.5 %all-to-all-start.1 = ((f32[512,1,2,192]{3,2,1,0:T(2,128)}), f32[512,1,2,192]{3,2,1,0:T(2,128)S(1)}, u32[]{:S(2)}, u32[]{:S(2)}) async-start(f32[512,1,2,192]{3,2,1,0:T(2,128)} %copy.19), calls=%async_computation.1 | async-start | bytes 2097152 | tf_op jit(solution)/shard_map/all_to_all | solution.py:68
  227.4 0.0 copy-start.1
  227.5 1.2 fusion.65
  228.7 2.4 convolution_bitcast_fusion
  231.1 0.0 copy-done.1
  231.1 1.3 convolution_bitcast_fusion.1
  232.4 4.4 %maximum_multiply_fusion = f32[1,2,1024,1024]{3,2,1,0:T(8,128)} fusion(f32[1,1,1024,1024]{3,2,1,0:T(8,128)S(1)} %convolution_bitcast_fusion, f32[1,1,1024,1024]{3,2,1,0:T(8,128)S(1)} %convolution_bitcast_fusion.1), kind=kLoop, calls=%fused_computation.3 | loop fusion | flops 4194304 | bytes 16777216 | tf_op jit(solution)/shard_map/div | solution.py:58
  236.8 8.6 %all-to-all-done.1 = f32[512,1,2,192]{3,2,1,0:T(2,128)S(1)} async-done(((f32[512,1,2,192]{3,2,1,0:T(2,128)}), f32[512,1,2,192]{3,2,1,0:T(2,128)S(1)}, u32[]{:S(2)}, u32[]{:S(2)}) %all-to-all-start.1) | async-done | bytes 786464 | tf_op jit(solution)/shard_map/all_to_all | solution.py:68
  245.4 0.1 copy.20
  245.5 1.8 copy.21
  (6 shorter events, 0.1 us)
Async XLA Ops:
  0.6 163.9 %copy-start = (f32[512,1024]{1,0:T(8,128)S(1)}, f32[512,1024]{1,0:T(8,128)}, u32[]{:S(2)}) copy-start(f32[512,1024]{1,0:T(8,128)} %param.9) | copy-start | bytes 6291460
  1.9 15.8 %copy-start.4 = (s32[128]{0:T(128)S(1)}, s32[128]{0:T(128)}, u32[]{:S(2)}) copy-start(s32[128]{0:T(128)} %param.6) | copy-start | bytes 1540
  135.4 27.8 %copy-start.3 = (s32[512]{0:T(512)S(1)}, s32[512]{0:T(512)}, u32[]{:S(2)}) copy-start(s32[512]{0:T(512)} %param.8) | copy-start | bytes 6148
  151.8 35.0 %all-to-all-start = ((bf16[128,2,1536]{2,1,0:T(2,128)(2,1)}), bf16[128,2,1536]{2,1,0:T(2,128)(2,1)S(1)}, u32[]{:S(2)}, u32[]{:S(2)}) async-start(bf16[128,2,1536]{2,1,0:T(2,128)(2,1)} %reshape.319), calls=%async_computation | async-start | bytes 1572864 | tf_op jit(solution)/shard_map/all_to_all | solution.py:49
  167.2 19.6 %copy-start.2 = (s32[1024]{0:T(1024)S(1)}, s32[1024]{0:T(1024)}, u32[]{:S(2)}) copy-start(s32[1024]{0:T(1024)} %param.7) | copy-start | bytes 12292
  217.9 27.5 %all-to-all-start.1 = ((f32[512,1,2,192]{3,2,1,0:T(2,128)}), f32[512,1,2,192]{3,2,1,0:T(2,128)S(1)}, u32[]{:S(2)}, u32[]{:S(2)}) async-start(f32[512,1,2,192]{3,2,1,0:T(2,128)} %copy.19), calls=%async_computation.1 | async-start | bytes 2097152 | tf_op jit(solution)/shard_map/all_to_all | solution.py:68
  227.4 3.7 %copy-start.1 = (bf16[2,1024,192]{1,2,0:T(8,128)(2,1)S(1)}, bf16[2,1024,192]{1,2,0:T(8,128)(2,1)}, u32[]{:S(2)}) copy-start(bf16[2,1024,192]{1,2,0:T(8,128)(2,1)} %fusion.28) | copy-start | bytes 2359300
where the time goes:
time: 248 us; the launch traced here: 247 us
  other arithmetic  145 us (58%)
  local copies, waits for them, and re-layouts  56 us (23%)
  starting transfers between devices  20.9 us (8%)
  matrix products  15.1 us (6%)
  waiting for transfers between devices  8.58 us (3%)
    convert_element_type x1, other arithmetic, filter_bank(): return total.astype(jnp.bfloat16)  109 us
    another operation x1, local copies, waits for them, and re-layouts, body(): samples = voltages[0].reshape(signals_dev, frames + TAPS - 1, NFFT)  15.8 us
    all_to_all x1, starting transfers between devices, body(): lax.all_to_all(spectra[:, :, None], ('tm', 'freq'), split_axis=0, concat_...  11.4 us
    gather x2, local copies, waits for them, and re-layouts, body(): volts = jnp.take(moved, antenna_map, axis=1)  10.9 us
    unnamed x13, local copies, waits for them, and re-layouts  10.8 us
    all_to_all x1, starting transfers between devices, body(): lax.all_to_all(formed[:, None], 'freq', split_axis=0, concat_axis=1, tile...  9.54 us
    reshape x2, local copies, waits for them, and re-layouts, body(): moved = moved.reshape(2, freq_count * signals_dev, tm_count * frames)  9.21 us
    another operation x1, other arithmetic  9.05 us
  transfers between devices with their start and end apart: 2, of which 1 were waited for; matrix products, arithmetic and copies ran while one was open for 13% of the time, Pallas kernels for 0%

commit v1 on v0

v1 whole, which is shorter than its diff:
```python
import functools
import math

import jax
import jax.numpy as jnp
import numpy as np
from jax import lax
from jax.experimental import pallas as pl
from jax.experimental.pallas import tpu as pltpu
from jax.sharding import PartitionSpec as P

NFFT = 4096
TAPS = 16
JB = 16
CHUNKS = 3
TM = 4
FREQ = 32
NDEV = TM * FREQ
SIGD = 32
CHAN = 128
BEAMS = 512
ANT = 1024
CENTRAL = (7, 8)
MESH = pl.DeviceIdType.MESH
f32 = jnp.float32
bf16 = jnp.bfloat16
i32 = jnp.int32


def prototype():
    total = TAPS * NFFT
    offsets = np.arange(total, dtype=np.float64)
    shifted = (offsets - 0.5 * total + 0.5) / NFFT
    window = 0.5 - 0.5 * np.cos(2.0 * math.pi / total * (offsets + 0.5))
    return (np.sinc(shifted) * window).reshape(TAPS, NFFT).astype(np.float32)


def turns(u):
    whole = jnp.floor(u + 0.5)
    theta = (u - whole) * (0.5 * math.pi)
    sq = theta * theta
    sin = theta * (1.0 + sq * (-1.0 / 6 + sq * (1.0 / 120 + sq * (-1.0 / 5040 + sq * (1.0 / 362880)))))
    cos = 1.0 + sq * (-0.5 + sq * (1.0 / 24 + sq * (-1.0 / 720 + sq * (1.0 / 40320))))
    quad = whole.astype(i32)
    odd = (quad & 1) != 0
    cos_out = jnp.where(odd, sin, cos)
    sin_out = jnp.where(odd, cos, sin)
    cos_out = jnp.where(((quad + 1) & 2) != 0, -cos_out, cos_out)
    sin_out = jnp.where((quad & 2) != 0, -sin_out, sin_out)
    return cos_out, sin_out


def column(row):
    return jnp.broadcast_to(row, (128, 128)).T


def lane_iota(rows=128, cols=128):
    return lax.broadcasted_iota(i32, (rows, cols), 1)


def main_kernel(
    v_hbm, taps_ref, bins_row, bins_smem, map_row, beam_row, delays_hbm,
    series_ref, beams_ref,
    vbuf, taps_b, table, filtered, spread, stage, recv, delays, weights, select, beam_sel,
    half, turned, xt, stage2, recv2, lanes_map,
    v_sem, d_sem, send_sem, recv_sem, send2_sem, recv2_sem,
):
    me_tm, me_f = lax.axis_index("tm"), lax.axis_index("freq")
    me = me_tm * FREQ + me_f
    barrier = pltpu.get_barrier_semaphore()

    first = JB + TAPS - 1
    quarter = NFFT // 4

    @pl.loop(0, 4)
    def _(nq):
        @pl.loop(0, first)
        def _(f):
            at = pl.ds(pl.multiple_of(f * NFFT + nq * quarter, quarter), quarter)
            pltpu.make_async_copy(v_hbm.at[0, :, at], vbuf.at[:, at], v_sem.at[nq]).start()

    for more in range(CHUNKS - 1):
        at = pl.ds((first + more * JB) * NFFT, JB * NFFT)
        pltpu.make_async_copy(v_hbm.at[0, :, at], vbuf.at[:, at], v_sem.at[4 + more]).start()
    delay_copy = pltpu.make_async_copy(delays_hbm, delays, d_sem)
    delay_copy.start()

    @pl.loop(1, NDEV)
    def _(i):
        peer = lax.rem(me + i, NDEV)
        pl.semaphore_signal(barrier, inc=1, device_id=(peer // FREQ, lax.rem(peer, FREQ)), device_id_type=MESH)

    @pl.loop(0, NFFT // 256)
    def _(nb):
        at = pl.ds(pl.multiple_of(nb * 256, 256), 256)
        for k in range(TAPS):
            taps_b[k, :, at] = jnp.broadcast_to(taps_ref[k : k + 1, at], (8, 256)).astype(bf16)

    bins_col = column(bins_row[...].astype(f32)).astype(i32)
    low_cos, low_sin = turns(((bins_col * lane_iota()) & (NFFT - 1)).astype(f32) * (4.0 / NFFT))
    high_cos, high_sin = turns(((bins_col * lane_iota()) & 31).astype(f32) * (4.0 / 32))
    scale = 1.0 / math.sqrt(NFFT)
    low_cos, low_sin = low_cos * scale, low_sin * scale
    for h in range(NFFT // 128):
        hc = jnp.broadcast_to(high_cos[:, h : h + 1], (128, 128))
        hs = jnp.broadcast_to(high_sin[:, h : h + 1], (128, 128))
        table[0:CHAN, h * 128 : (h + 1) * 128] = (low_cos * hc - low_sin * hs).astype(bf16)
        table[CHAN : 2 * CHAN, h * 128 : (h + 1) * 128] = (-(low_sin * hc + low_cos * hs)).astype(bf16)

    def filter_block(jc, nb, rb):
        c0 = pl.multiple_of(nb * 256, 256)
        at = pl.ds(c0, 256)
        outer = {k: taps_b[k, :, at] for k in range(TAPS) if k not in CENTRAL}
        central = {k: jnp.broadcast_to(taps_ref[k : k + 1, at], (8, 256)) for k in CENTRAL}
        small = [None] * JB
        large = [None] * JB
        for i in range(JB + TAPS - 1):
            x = vbuf[rb * 8 : (rb + 1) * 8, pl.ds(pl.multiple_of((jc * JB + i) * NFFT + c0, 256), 256)]
            wide = None
            for j in range(max(0, i - TAPS + 1), min(JB - 1, i) + 1):
                k = i - j
                if k in CENTRAL:
                    wide = x.astype(f32) if wide is None else wide
                    term = central[k] * wide
                    large[j] = term if large[j] is None else large[j] + term
                else:
                    term = outer[k] * x
                    small[j] = term if small[j] is None else small[j] + term
            j = i - TAPS + 1
            if j >= 0:
                filtered[rb * 128 + j * 8 : rb * 128 + (j + 1) * 8, at] = (large[j] + small[j].astype(f32)).astype(bf16)

    @pl.loop(0, CHUNKS)
    def _(jc):
        @pl.when(jc > 0)
        def _():
            at = pl.ds(0, JB * NFFT)
            pltpu.make_async_copy(v_hbm.at[0, :, at], vbuf.at[:, at], v_sem.at[3 + jc]).wait()

        @pl.loop(0, NFFT // 256)
        def _(nb):
            @pl.when((jc == 0) & (lax.rem(nb, 4) == 0))
            def _():
                at = pl.ds(0, first * quarter)
                pltpu.make_async_copy(v_hbm.at[0, :, at], vbuf.at[:, at], v_sem.at[nb // 4]).wait()

            for rb in range(SIGD // 8):
                filter_block(jc, nb, rb)

        for nt in range(2):
            out = lax.dot_general(
                table[...], filtered[nt * 256 : (nt + 1) * 256, :], (((1,), (1,)), ((), ())), preferred_element_type=f32
            )
            for r in range(2):
                for part in range(2):
                    rb = nt * 2 + part
                    spread[pl.ds(rb * 2 + r, CHAN, stride=8), :] = out[r * CHAN : (r + 1) * CHAN, part * 128 : (part + 1) * 128]

        @pl.loop(0, CHAN // 16)
        def _(cb):
            for i in range(16):
                c = cb * 16 + i
                stage[jc, c] = spread[pl.ds(pl.multiple_of(c * 8, 8), 8), :].astype(bf16)

        @pl.when(jc == 0)
        def _():
            pl.semaphore_wait(barrier, NDEV - 1)

        pltpu.make_async_copy(stage.at[jc, me], recv.at[jc, me], recv_sem.at[jc]).start()

        @pl.loop(1, NDEV)
        def _(i):
            peer = lax.rem(me + i, NDEV)
            pltpu.make_async_remote_copy(
                src_ref=stage.at[jc, peer], dst_ref=recv.at[jc, me], send_sem=send_sem.at[jc], recv_sem=recv_sem.at[jc],
                device_id=(peer // FREQ, lax.rem(peer, FREQ)), device_id_type=MESH,
            ).start()

    delay_copy.wait()
    bin_value = bins_smem[me].astype(f32)

    @pl.loop(0, BEAMS // 32)
    def _(pb):
        row = pl.multiple_of(pb * 32, 32)
        for part in range(4):
            cos, sin = turns(delays[pl.ds(row, 32), part * 256 : (part + 1) * 256] * bin_value * (4.0 / NFFT))
            weights[pl.ds(row, 32), part * 256 : (part + 1) * 256] = cos.astype(bf16)
            weights[pl.ds(BEAMS + row, 32), part * 256 : (part + 1) * 256] = sin.astype(bf16)

    lanes = lane_iota()
    signal = (lanes // 4) * SIGD + lax.rem(lanes, 4) * 8
    for ab in range(ANT // 128):
        wanted = column(map_row[:, ab * 128 : (ab + 1) * 128].astype(f32)).astype(i32)
        for s8 in range(8):
            select[ab * 128 : (ab + 1) * 128, s8 * 128 : (s8 + 1) * 128] = jnp.where(wanted == signal + s8, 1.0, 0.0).astype(bf16)
    for bb in range(BEAMS // 128):
        wanted = column(beam_row[:, bb * 128 : (bb + 1) * 128].astype(f32)).astype(i32)
        for pb in range(BEAMS // 128):
            beam_sel[bb * 128 : (bb + 1) * 128, pb * 128 : (pb + 1) * 128] = jnp.where(wanted == lanes + pb * 128, 1.0, 0.0).astype(bf16)
    for jc in range(CHUNKS):
        rows = lax.broadcasted_iota(i32, (128, 384), 0)
        to = (rows // 64) * 192 + (lax.rem(rows, 64) // 16) * 48 + jc * JB + lax.rem(rows, 16)
        lanes_map[jc * 128 : (jc + 1) * 128, :] = jnp.where(to == lane_iota(128, 384), 1.0, 0.0).astype(bf16)

    @pl.loop(0, CHUNKS)
    def _(jc):
        pltpu.make_async_copy(stage.at[jc], recv.at[jc], recv_sem.at[jc]).wait()

        @pl.loop(0, TM)
        def _(q):
            for f in range(FREQ):
                half[f * 8 : (f + 1) * 8, :] = recv[jc, q * FREQ + f].astype(f32)
            for r in range(2):
                turned[...] = half[pl.ds(r, 128, stride=2), :].T
                row = pl.multiple_of((r * TM + q) * JB, JB)
                for s8 in range(8):
                    xt[pl.ds(row, JB), s8 * 128 : (s8 + 1) * 128] = turned[pl.ds(s8, JB, stride=8), :].astype(bf16)

        at = pl.ds(pl.multiple_of(jc * 128, 128), 128)

        @pl.loop(0, ANT // 256)
        def _(ab):
            rows = pl.ds(pl.multiple_of(ab * 256, 256), 256)
            series_ref[rows, at] = lax.dot_general(
                select[rows, :], xt[...], (((1,), (1,)), ((), ())), preferred_element_type=f32
            ).astype(bf16)

        series = series_ref[:, at]
        sign = jnp.where(lane_iota(BEAMS // 2, 128) < 64, 1.0, -1.0)
        formed = []
        for pb in range(2):
            cos_part = jnp.dot(weights[pb * 256 : (pb + 1) * 256, :], series, preferred_element_type=f32)
            sin_part = jnp.dot(weights[BEAMS + pb * 256 : BEAMS + (pb + 1) * 256, :], series, preferred_element_type=f32)
            formed.append(((cos_part + sign * pltpu.roll(sin_part, 64, 1)) * (1.0 / math.sqrt(ANT))).astype(bf16))
        picked = jnp.dot(beam_sel[...], jnp.concatenate(formed, 0), preferred_element_type=f32).astype(bf16)
        stage2[jc] = picked.reshape(FREQ, 16, 128)

        pltpu.make_async_copy(stage2.at[jc, me_f], recv2.at[jc, me_f], recv2_sem.at[jc]).start()

        @pl.loop(1, FREQ)
        def _(i):
            peer = lax.rem(me_f + i, FREQ)
            pltpu.make_async_remote_copy(
                src_ref=stage2.at[jc, peer], dst_ref=recv2.at[jc, me_f], send_sem=send2_sem.at[jc], recv_sem=recv2_sem.at[jc],
                device_id=(me_tm, peer), device_id_type=MESH,
            ).start()

    for jc in range(CHUNKS):
        pltpu.make_async_copy(stage2.at[jc], recv2.at[jc], recv2_sem.at[jc]).wait()

    @pl.loop(0, FREQ // 8)
    def _(cb):
        total = None
        for jc in range(CHUNKS):
            part = recv2[jc, pl.ds(cb * 8, 8)].reshape(128, 128)
            term = jnp.dot(part, lanes_map[jc * 128 : (jc + 1) * 128, :], preferred_element_type=f32)
            total = term if total is None else total + term
        beams_ref[pl.ds(cb * 128, 128), :] = total

    for jc in range(CHUNKS):
        sent = stage.at[jc, pl.ds(0, NDEV - 1)]
        pltpu.make_async_copy(sent, sent, send_sem.at[jc]).wait()
        sent = stage2.at[jc, pl.ds(0, FREQ - 1)]
        pltpu.make_async_copy(sent, sent, send2_sem.at[jc]).wait()


def vis_kernel(rows_ref, all_ref, out_ref):
    rows = rows_ref[...]
    every = all_ref[...]
    nt = (((1,), (1,)), ((), ()))
    scale = 1.0 / 192.0
    out_ref[0, 0] = lax.dot_general(rows, every, nt, preferred_element_type=f32) * scale
    parts = []
    for jc in range(CHUNKS):
        part = rows[:, jc * 128 : (jc + 1) * 128].astype(f32)
        sign = jnp.where(lane_iota(*part.shape) < 64, 1.0, -1.0)
        parts.append((pltpu.roll(part, 64, 1) * sign).astype(bf16))
    swapped = jnp.concatenate(parts, 1)
    out_ref[0, 1] = lax.dot_general(swapped, every, nt, preferred_element_type=f32) * scale


def body(voltages, chan_bins, antenna_map, beam_index, delays):
    vmem = pl.BlockSpec(memory_space=pltpu.VMEM)
    anywhere = pl.BlockSpec(memory_space=pl.ANY)
    dma = pltpu.SemaphoreType.DMA
    series, beams = pl.pallas_call(
        main_kernel,
        out_shape=(
            jax.ShapeDtypeStruct((ANT, 384), bf16),
            jax.ShapeDtypeStruct((FREQ * 16, 384), f32),
        ),
        in_specs=[anywhere, vmem, vmem, pl.BlockSpec(memory_space=pltpu.SMEM), vmem, vmem, anywhere],
        out_specs=(vmem, vmem),
        scratch_shapes=[
            pltpu.VMEM((SIGD, 63 * NFFT), bf16),
            pltpu.VMEM((TAPS, 8, NFFT), bf16),
            pltpu.VMEM((2 * CHAN, NFFT), bf16),
            pltpu.VMEM((SIGD * JB, NFFT), bf16),
            pltpu.VMEM((CHAN * 8, 128), f32),
            pltpu.VMEM((CHUNKS, NDEV, 8, 128), bf16),
            pltpu.VMEM((CHUNKS, NDEV, 8, 128), bf16),
            pltpu.VMEM((BEAMS, ANT), f32),
            pltpu.VMEM((2 * BEAMS, ANT), bf16),
            pltpu.VMEM((ANT, ANT), bf16),
            pltpu.VMEM((BEAMS, BEAMS), bf16),
            pltpu.VMEM((256, 128), f32),
            pltpu.VMEM((128, 128), f32),
            pltpu.VMEM((128, ANT), bf16),
            pltpu.VMEM((CHUNKS, FREQ, 16, 128), bf16),
            pltpu.VMEM((CHUNKS, FREQ, 16, 128), bf16),
            pltpu.VMEM((384, 384), bf16),
            dma((6,)),
            dma,
            dma((CHUNKS,)),
            dma((CHUNKS,)),
            dma((CHUNKS,)),
            dma((CHUNKS,)),
        ],
        compiler_params=pltpu.CompilerParams(
            collective_id=0, has_side_effects=True, vmem_limit_bytes=60 * 1024 * 1024
        ),
        name="channelize",
    )(
        voltages,
        jnp.asarray(prototype()),
        chan_bins.reshape(1, CHAN),
        chan_bins,
        antenna_map.reshape(1, ANT),
        beam_index.reshape(1, BEAMS),
        delays,
    )
    block = 128
    visibilities = pl.pallas_call(
        vis_kernel,
        grid=(ANT // block,),
        out_shape=jax.ShapeDtypeStruct((1, 2, ANT, ANT), f32),
        in_specs=[pl.BlockSpec((block, 384), lambda i: (i, 0)), pl.BlockSpec((ANT, 384), lambda i: (0, 0))],
        out_specs=pl.BlockSpec((1, 2, block, ANT), lambda i: (0, 0, i, 0)),
        name="correlate",
    )(series, series)
    beam_volts = beams.reshape(FREQ, 16, 2, 192).transpose(1, 0, 2, 3)
    return (visibilities, beam_volts)


def solution(mesh):
    return jax.shard_map(
        body,
        mesh=mesh,
        in_specs=(P("tm", "freq", None), P(), P(), P(), P()),
        out_specs=(P(("tm", "freq"), None, None, None), P("freq", "tm", None, None)),
        check_vma=False,
    )
```

time: 248 us -> 75.9 us (0.31)
  other arithmetic: 145 us -> 0 us
  Pallas kernels: 0 us -> 71.5 us
  local copies, waits for them, and re-layouts: 56 us -> 3.39 us
  starting transfers between devices: 20.9 us -> 0 us
  matrix products: 15.1 us -> 0 us
  waiting for transfers between devices: 8.58 us -> 0 us
    convert_element_type x2 -> x0, other arithmetic: 117 us -> none  [the longest x1 109 us: filter_bank(): return total.astype(jnp.bfloat16)]
    pallas_call x0 -> x2, Pallas kernels: none -> 71.5 us  [the longest x1 62.7 us: body(): pl.pallas_call(main_kernel, out_shape=(jax.ShapeDtypeStruct((ANT, 384), b...]
    all_to_all x2 -> x0, starting transfers between devices: 20.9 us -> none  [the longest x1 11.4 us: body(): lax.all_to_all(spectra[:, :, None], ('tm', 'freq'), split_axis=0, concat_...]
    another operation x2 -> x0, local copies, waits for them, and re-layouts: 19.5 us -> none  [the longest x1 15.8 us: body(): samples = voltages[0].reshape(signals_dev, frames + TAPS - 1, NFFT)]
    dot_general x4 -> x0, matrix products: 15.1 us -> none  [the longest x1 6.78 us: body(): jnp.einsum('rcn,mn->crm', table, filtered, preferred_element_type=jnp.flo...]
    gather x3 -> x0, local copies, waits for them, and re-layouts: 13.6 us -> none  [the longest x2 10.9 us: body(): volts = jnp.take(moved, antenna_map, axis=1)]
    another operation x2 -> x0, other arithmetic: 11.4 us -> none
    unnamed x13 -> x0, local copies, waits for them, and re-layouts: 10.8 us -> none
  transfers between devices with their start and end apart: 2 -> 0, of which waited for: 1 -> 0; matrix products, arithmetic and copies ran while one was open for 13% -> 0% of each run, Pallas kernels for 0% -> 0%
where the time goes in v1:
time: 75.9 us; the launch traced here: 75.5 us
  Pallas kernels  71.5 us (94%)
  local copies, waits for them, and re-layouts  3.39 us (4%)
    pallas_call x1, Pallas kernels, body(): pl.pallas_call(main_kernel, out_shape=(jax.ShapeDtypeStruct((ANT, 384), b...  62.7 us
    pallas_call x1, Pallas kernels, body(): pl.pallas_call(vis_kernel, grid=(ANT // block,), out_shape=jax.ShapeDtype...  8.77 us
    reshape x2, local copies, waits for them, and re-layouts, body(): beam_volts = beams.reshape(FREQ, 16, 2, 192).transpose(1, 0, 2, 3)  3.39 us

profile of v1, /device:TPU:0, one launch (start us, length us, event | category | flops | bytes accessed | tf_op | source)
XLA Modules:
  0.0 75.5 jit_solution(8430098153094914793)
XLA Ops:
  0.6 62.7 %channelize.1 = (bf16[1024,384]{1,0:T(8,128)(2,1)}, f32[512,384]{1,0:T(8,128)}) custom-call(bf16[1,32,258048]{2,1,0:T(8,128)(2,1)} %v_hbm.1, f32[16,4096]{1,0:T(8,128)} %constant.2.clone.taps_ref, s32[1,128]{1,0:T(1,128)} %bitcast.9, s32[128]{0:T(128)} %bins_smem.1, s32[1,1024]{1,0:T(1,128)} %bitcast.7, s32[1,512]{1,0:T(1,128)} %bitcast.8, ...), custom_call_target="tpu_custom_call" | custom-call | tf_op jit(solution)/shard_map/channelize/pallas_call | solution.py:286
  63.3 1.9 %reshape.19 = f32[32,16,2,192]{3,2,1,0:T(2,128)S(1)} reshape(f32[512,384]{1,0:T(8,128)} %get-tuple-element.5) | data formatting | bytes 1572864 | tf_op jit(solution)/shard_map/reshape | solution.py:341
  65.2 1.5 %copy.10 = f32[32,16,2,192]{3,2,0,1:T(2,128)} copy(f32[32,16,2,192]{3,2,1,0:T(2,128)S(1)} %reshape.19) | data formatting | bytes 1572864 | tf_op jit(solution)/shard_map/reshape | solution.py:341
  66.7 8.8 %correlate.1 = f32[1,2,1024,1024]{3,2,1,0:T(8,128)} custom-call(bf16[1024,384]{1,0:T(8,128)(2,1)} %get-tuple-element.4.rows_ref.all_ref, bf16[1024,384]{1,0:T(8,128)(2,1)} %get-tuple-element.4.rows_ref.all_ref), custom_call_target="tpu_custom_call" | custom-call | tf_op jit(solution)/shard_map/correlate/pallas_call | solution.py:333

commit v2 on v1

v2 whole, which is shorter than its diff:
```python
import functools
import math

import jax
import jax.numpy as jnp
import numpy as np
from jax import lax
from jax.experimental import pallas as pl
from jax.experimental.pallas import tpu as pltpu
from jax.sharding import PartitionSpec as P

NFFT = 4096
TAPS = 16
JB = 16
CHUNKS = 3
TM = 4
FREQ = 32
NDEV = TM * FREQ
SIGD = 32
CHAN = 128
BEAMS = 512
ANT = 1024
CENTRAL = (7, 8)
EACH = 7
VSTEPS = 4
VMEM_LIMIT = 60 * 1024 * 1024
MESH = pl.DeviceIdType.MESH
f32 = jnp.float32
bf16 = jnp.bfloat16
i32 = jnp.int32


def prototype():
    total = TAPS * NFFT
    offsets = np.arange(total, dtype=np.float64)
    shifted = (offsets - 0.5 * total + 0.5) / NFFT
    window = 0.5 - 0.5 * np.cos(2.0 * math.pi / total * (offsets + 0.5))
    return (np.sinc(shifted) * window).reshape(TAPS, NFFT).astype(np.float32)


def turns(u):
    whole = jnp.floor(u + 0.5)
    theta = (u - whole) * (0.5 * math.pi)
    sq = theta * theta
    sin = theta * (1.0 + sq * (-1.0 / 6 + sq * (1.0 / 120 + sq * (-1.0 / 5040 + sq * (1.0 / 362880)))))
    cos = 1.0 + sq * (-0.5 + sq * (1.0 / 24 + sq * (-1.0 / 720 + sq * (1.0 / 40320))))
    quad = whole.astype(i32)
    odd = (quad & 1) != 0
    cos_out = jnp.where(odd, sin, cos)
    sin_out = jnp.where(odd, cos, sin)
    cos_out = jnp.where(((quad + 1) & 2) != 0, -cos_out, cos_out)
    sin_out = jnp.where((quad & 2) != 0, -sin_out, sin_out)
    return cos_out, sin_out


def column(row):
    return jnp.broadcast_to(row, (128, 128)).T


def lane_iota(rows=128, cols=128):
    return lax.broadcasted_iota(i32, (rows, cols), 1)


def main_kernel(
    v_hbm, taps_hbm, bins_hbm, bins_smem, map_hbm, beam_hbm, delays_hbm,
    series_hbm, beams_hbm,
    vbuf, taps_ref, bins_row, map_row, beam_row, taps_b, table, filtered, spread, stage, recv, delays, weights, select, beam_sel,
    half, turned, xt, series, stage2,
    v_sem, small_sem, d_sem, send_sem, recv_sem, send2_sem, recv2_sem, out_sem,
):
    me_tm, me_f = lax.axis_index("tm"), lax.axis_index("freq")
    me = me_tm * FREQ + me_f
    barrier = pltpu.get_barrier_semaphore()

    def peer_id(i):
        peer = (me + i) & (NDEV - 1)
        return peer, (peer >> 5, peer & (FREQ - 1))

    def greet(i):
        pl.semaphore_signal(barrier, inc=1, device_id=peer_id(i)[1], device_id_type=MESH)

    def send(jc, i):
        peer, where = peer_id(i)
        pltpu.make_async_remote_copy(
            src_ref=stage.at[jc, peer], dst_ref=recv.at[jc, me], send_sem=send_sem.at[jc], recv_sem=recv_sem.at[jc],
            device_id=where, device_id_type=MESH,
        ).start()

    def ahead(act):
        @pl.loop(1, NDEV - 16 * EACH)
        def _(i):
            act(i)

    def beside(step, act):
        for u in range(EACH):
            act(NDEV - 16 * EACH + step * EACH + u)

    first = JB + TAPS - 1
    quarter = NFFT // 4

    def fetch_quarter(nq):
        @pl.loop(0, first)
        def _(f):
            at = pl.ds(pl.multiple_of(f * NFFT + nq * quarter, quarter), quarter)
            pltpu.make_async_copy(v_hbm.at[0, :, at], vbuf.at[:, at], v_sem.at[nq]).start()

    smalls = [
        pltpu.make_async_copy(src, dst, small_sem.at[n])
        for n, (src, dst) in enumerate(((taps_hbm, taps_ref), (bins_hbm, bins_row), (map_hbm, map_row), (beam_hbm, beam_row)))
    ]
    for small in smalls:
        small.start()
    fetch_quarter(0)
    smalls[0].wait()

    @pl.loop(0, NFFT // 256)
    def _(nb):
        at = pl.ds(pl.multiple_of(nb * 256, 256), 256)
        for k in range(TAPS):
            taps_b[k, :, at] = jnp.broadcast_to(taps_ref[k : k + 1, at], (8, 256)).astype(bf16)

    @pl.loop(1, 4)
    def _(nq):
        fetch_quarter(nq)

    for more in range(CHUNKS - 1):
        at = pl.ds((first + more * JB) * NFFT, JB * NFFT)
        pltpu.make_async_copy(v_hbm.at[0, :, at], vbuf.at[:, at], v_sem.at[4 + more]).start()
    delay_copy = pltpu.make_async_copy(delays_hbm, delays, d_sem)
    delay_copy.start()

    for small in smalls[1:]:
        small.wait()
    bins_col = column(bins_row[...].astype(f32)).astype(i32)
    low_cos, low_sin = turns(((bins_col * lane_iota()) & (NFFT - 1)).astype(f32) * (4.0 / NFFT))
    high_cos, high_sin = turns(((bins_col * lane_iota()) & 31).astype(f32) * (4.0 / 32))
    scale = 1.0 / math.sqrt(NFFT)
    low_cos, low_sin = low_cos * scale, low_sin * scale
    for h in range(NFFT // 128):
        hc = jnp.broadcast_to(high_cos[:, h : h + 1], (128, 128))
        hs = jnp.broadcast_to(high_sin[:, h : h + 1], (128, 128))
        table[0:CHAN, h * 128 : (h + 1) * 128] = (low_cos * hc - low_sin * hs).astype(bf16)
        table[CHAN : 2 * CHAN, h * 128 : (h + 1) * 128] = (-(low_sin * hc + low_cos * hs)).astype(bf16)

    def filter_block(jc, nb, rb):
        c0 = pl.multiple_of(nb * 256, 256)
        at = pl.ds(c0, 256)
        outer = {k: taps_b[k, :, at] for k in range(TAPS) if k not in CENTRAL}
        central = {k: jnp.broadcast_to(taps_ref[k : k + 1, at], (8, 256)) for k in CENTRAL}
        small = [None] * JB
        large = [None] * JB
        for i in range(JB + TAPS - 1):
            x = vbuf[rb * 8 : (rb + 1) * 8, pl.ds(pl.multiple_of((jc * JB + i) * NFFT + c0, 256), 256)]
            wide = None
            for j in range(max(0, i - TAPS + 1), min(JB - 1, i) + 1):
                k = i - j
                if k in CENTRAL:
                    wide = x.astype(f32) if wide is None else wide
                    term = central[k] * wide
                    large[j] = term if large[j] is None else large[j] + term
                else:
                    term = outer[k] * x
                    small[j] = term if small[j] is None else small[j] + term
            j = i - TAPS + 1
            if j >= 0:
                filtered[rb * 128 + j * 8 : rb * 128 + (j + 1) * 8, at] = (large[j] + small[j].astype(f32)).astype(bf16)

    def channelize(jc, act):
        if jc > 0:
            at = pl.ds(0, JB * NFFT)
            pltpu.make_async_copy(v_hbm.at[0, :, at], vbuf.at[:, at], v_sem.at[3 + jc]).wait()
        ahead(act)
        @pl.loop(0, NFFT // 256)
        def _(nb):
            if jc == 0:
                @pl.when(lax.rem(nb, 4) == 0)
                def _():
                    at = pl.ds(0, first * quarter)
                    pltpu.make_async_copy(v_hbm.at[0, :, at], vbuf.at[:, at], v_sem.at[nb // 4]).wait()

            beside(nb, act)
            for rb in range(SIGD // 8):
                filter_block(jc, nb, rb)

        for nt in range(2):
            out = lax.dot_general(
                table[...], filtered[nt * 256 : (nt + 1) * 256, :], (((1,), (1,)), ((), ())), preferred_element_type=f32
            )
            for r in range(2):
                for part in range(2):
                    rb = nt * 2 + part
                    spread[pl.ds(rb * 2 + r, CHAN, stride=8), :] = out[r * CHAN : (r + 1) * CHAN, part * 128 : (part + 1) * 128]

        @pl.loop(0, CHAN // 16)
        def _(cb):
            for i in range(16):
                c = cb * 16 + i
                stage[jc, c] = spread[pl.ds(pl.multiple_of(c * 8, 8), 8), :].astype(bf16)

        if jc == 0:
            pl.semaphore_wait(barrier, NDEV - 1)
        pltpu.make_async_copy(stage.at[jc, me], recv.at[jc, me], recv_sem.at[jc]).start()

    channelize(0, greet)
    channelize(1, functools.partial(send, 0))
    channelize(2, functools.partial(send, 1))

    delay_copy.wait()
    bin_value = bins_smem[me].astype(f32) * (4.0 / NFFT)

    ahead(functools.partial(send, 2))

    @pl.loop(0, BEAMS // 32)
    def _(pb):
        beside(pb, functools.partial(send, 2))
        row = pl.multiple_of(pb * 32, 32)
        for part in range(4):
            cos, sin = turns(delays[pl.ds(row, 32), part * 256 : (part + 1) * 256] * bin_value)
            weights[pl.ds(row, 32), part * 256 : (part + 1) * 256] = cos.astype(bf16)
            weights[pl.ds(BEAMS + row, 32), part * 256 : (part + 1) * 256] = sin.astype(bf16)

    lanes = lane_iota()
    signal = (lanes // 4) * SIGD + lax.rem(lanes, 4) * 8
    for ab in range(ANT // 128):
        wanted = column(map_row[:, ab * 128 : (ab + 1) * 128].astype(f32)).astype(i32)
        for s8 in range(8):
            select[ab * 128 : (ab + 1) * 128, s8 * 128 : (s8 + 1) * 128] = jnp.where(wanted == signal + s8, 1.0, 0.0).astype(bf16)
    for bb in range(BEAMS // 128):
        wanted = column(beam_row[:, bb * 128 : (bb + 1) * 128].astype(f32)).astype(i32)
        for pb in range(BEAMS // 128):
            beam_sel[bb * 128 : (bb + 1) * 128, pb * 128 : (pb + 1) * 128] = jnp.where(wanted == lanes + pb * 128, 1.0, 0.0).astype(bf16)
    def beamform(low, high):
        for jc in range(low, high):
            pltpu.make_async_copy(stage.at[jc], recv.at[jc], recv_sem.at[jc]).wait()

            @pl.loop(0, TM)
            def _(q):
                for f in range(FREQ):
                    half[f * 8 : (f + 1) * 8, :] = recv[jc, q * FREQ + f].astype(f32)
                for r in range(2):
                    turned[...] = half[pl.ds(r, 128, stride=2), :].T
                    row = pl.multiple_of((jc - low) * 128 + (r * TM + q) * JB, JB)
                    for s8 in range(8):
                        xt[pl.ds(row, JB), s8 * 128 : (s8 + 1) * 128] = turned[pl.ds(s8, JB, stride=8), :].astype(bf16)

        count = high - low
        cols = slice(low * 128, high * 128)

        @pl.loop(0, ANT // 256)
        def _(ab):
            rows = pl.ds(pl.multiple_of(ab * 256, 256), 256)
            series[rows, cols] = lax.dot_general(
                select[rows, :], xt[0 : count * 128, :], (((1,), (1,)), ((), ())), preferred_element_type=f32
            ).astype(bf16)

        pltpu.make_async_copy(series.at[:, cols], series_hbm.at[:, cols], out_sem.at[low]).start()
        ordered = series[:, cols]
        sign = jnp.where(lane_iota(BEAMS // 2, 128) < 64, 1.0 / math.sqrt(ANT), -1.0 / math.sqrt(ANT))
        formed = []
        for pb in range(2):
            cos_part = jnp.dot(weights[pb * 256 : (pb + 1) * 256, :], ordered, preferred_element_type=f32)
            sin_part = jnp.dot(weights[BEAMS + pb * 256 : BEAMS + (pb + 1) * 256, :], ordered, preferred_element_type=f32)
            turn = [sign * pltpu.roll(sin_part[:, n * 128 : (n + 1) * 128], 64, 1) for n in range(count)]
            formed.append((cos_part * (1.0 / math.sqrt(ANT)) + jnp.concatenate(turn, 1)).astype(bf16))
        picked = jnp.dot(beam_sel[...], jnp.concatenate(formed, 0), preferred_element_type=f32)
        for jc in range(low, high):
            part = picked[:, (jc - low) * 128 : (jc - low + 1) * 128]
            stage2[jc] = part.astype(bf16).reshape(FREQ, 16, 128)
            pltpu.make_async_copy(stage2.at[jc, me_f], beams_hbm.at[jc, me_f], recv2_sem.at[jc]).start()

            @pl.loop(1, FREQ)
            def _(i):
                peer = (me_f + i) & (FREQ - 1)
                pltpu.make_async_remote_copy(
                    src_ref=stage2.at[jc, peer], dst_ref=beams_hbm.at[jc, me_f], send_sem=send2_sem.at[jc],
                    recv_sem=recv2_sem.at[jc], device_id=(me_tm, peer), device_id_type=MESH,
                ).start()

    beamform(0, 2)
    beamform(2, 3)

    for jc in range(CHUNKS):
        sent = stage.at[jc, pl.ds(0, NDEV - 1)]
        pltpu.make_async_copy(sent, sent, send_sem.at[jc]).wait()
        sent = stage2.at[jc, pl.ds(0, FREQ - 1)]
        pltpu.make_async_copy(sent, sent, send2_sem.at[jc]).wait()
    for low, high in ((0, 2), (2, 3)):
        cols = slice(low * 128, high * 128)
        pltpu.make_async_copy(series.at[:, cols], series_hbm.at[:, cols], out_sem.at[low]).wait()
    for jc in range(CHUNKS):
        pltpu.make_async_copy(stage2.at[jc], beams_hbm.at[jc], recv2_sem.at[jc]).wait()


def vis_kernel(series_ref, part_ref, beams_ref, vis_ref, out_ref):
    part = part_ref[...]
    swapped = []
    for jc in range(CHUNKS):
        chunk = part[:, jc * 128 : (jc + 1) * 128].astype(f32)
        sign = jnp.where(lane_iota(*chunk.shape) < 64, 1.0, -1.0)
        swapped.append((pltpu.roll(chunk, 64, 1) * sign).astype(bf16))
    pair = jnp.concatenate([part, jnp.concatenate(swapped, 1)], 0)
    count = ANT // VSTEPS
    for bb in range(4):
        cols = slice(bb * 256, (bb + 1) * 256)
        out = lax.dot_general(pair, series_ref[cols, :], (((1,), (1,)), ((), ())), preferred_element_type=f32)
        out = out * (1.0 / 192.0)
        vis_ref[0, 0, :, cols] = out[:count]
        vis_ref[0, 1, :, cols] = out[count:]

    @pl.when(pl.program_id(0) == VSTEPS // 2)
    def _():
        moves = []
        for jc in range(CHUNKS):
            rows = lax.broadcasted_iota(i32, (128, 512), 0)
            to = (rows >> 6) * 256 + ((rows >> 4) & 3) * 48 + jc * JB + (rows & 15)
            moves.append(jnp.where(to == lane_iota(128, 512), 1.0, 0.0).astype(bf16))
        moves = jnp.concatenate(moves, 0)
        for cb in range(4):
            found = jnp.concatenate([beams_ref[jc, cb * 128 : (cb + 1) * 128, :] for jc in range(CHUNKS)], 1)
            total = jnp.dot(found, moves, preferred_element_type=f32)
            for u in range(8):
                for r in range(2):
                    rows = slice(u * 16, (u + 1) * 16)
                    out_ref[:, cb * 8 + u, r, 0:128] = total[rows, r * 256 : r * 256 + 128]
                    out_ref[:, cb * 8 + u, r, 128:192] = total[rows, r * 256 + 128 : r * 256 + 192]


def body(voltages, chan_bins, antenna_map, beam_index, delays):
    hbm = pl.BlockSpec(memory_space=pltpu.HBM)
    anywhere = pl.BlockSpec(memory_space=pl.ANY)
    dma = pltpu.SemaphoreType.DMA
    series, beams = pl.pallas_call(
        main_kernel,
        out_shape=(
            jax.ShapeDtypeStruct((ANT, 384), bf16),
            jax.ShapeDtypeStruct((CHUNKS, FREQ, 16, 128), bf16),
        ),
        in_specs=[hbm, hbm, hbm, pl.BlockSpec(memory_space=pltpu.SMEM), hbm, hbm, hbm],
        out_specs=(anywhere, anywhere),
        scratch_shapes=[
            pltpu.VMEM((SIGD, 63 * NFFT), bf16),
            pltpu.VMEM((TAPS, NFFT), f32),
            pltpu.VMEM((1, CHAN), i32),
            pltpu.VMEM((1, ANT), i32),
            pltpu.VMEM((1, BEAMS), i32),
            pltpu.VMEM((TAPS, 8, NFFT), bf16),
            pltpu.VMEM((2 * CHAN, NFFT), bf16),
            pltpu.VMEM((SIGD * JB, NFFT), bf16),
            pltpu.VMEM((CHAN * 8, 128), f32),
            pltpu.VMEM((CHUNKS, NDEV, 8, 128), bf16),
            pltpu.VMEM((CHUNKS, NDEV, 8, 128), bf16),
            pltpu.VMEM((BEAMS, ANT), f32),
            pltpu.VMEM((2 * BEAMS, ANT), bf16),
            pltpu.VMEM((ANT, ANT), bf16),
            pltpu.VMEM((BEAMS, BEAMS), bf16),
            pltpu.VMEM((256, 128), f32),
            pltpu.VMEM((128, 128), f32),
            pltpu.VMEM((256, ANT), bf16),
            pltpu.VMEM((ANT, 384), bf16),
            pltpu.VMEM((CHUNKS, FREQ, 16, 128), bf16),
            dma((6,)),
            dma((4,)),
            dma,
            dma((CHUNKS,)),
            dma((CHUNKS,)),
            dma((CHUNKS,)),
            dma((CHUNKS,)),
            dma((CHUNKS,)),
        ],
        compiler_params=pltpu.CompilerParams(
            collective_id=0, has_side_effects=True, vmem_limit_bytes=VMEM_LIMIT
        ),
        name="channelize",
    )(
        voltages,
        jnp.asarray(prototype()),
        chan_bins.reshape(1, CHAN),
        chan_bins,
        antenna_map.reshape(1, ANT),
        beam_index.reshape(1, BEAMS),
        delays,
    )
    rows = ANT // VSTEPS
    visibilities, beam_volts = pl.pallas_call(
        vis_kernel,
        grid=(VSTEPS,),
        out_shape=(
            jax.ShapeDtypeStruct((1, 2, ANT, ANT), f32),
            jax.ShapeDtypeStruct((16, FREQ, 2, 192), f32),
        ),
        in_specs=[
            pl.BlockSpec(memory_space=pltpu.VMEM),
            pl.BlockSpec((rows, 384), lambda i: (i, 0)),
            pl.BlockSpec(memory_space=pltpu.VMEM),
        ],
        out_specs=(
            pl.BlockSpec((1, 2, rows, ANT), lambda i: (0, 0, i, 0)),
            pl.BlockSpec((16, FREQ, 2, 192), lambda i: (0, 0, 0, 0)),
        ),
        compiler_params=pltpu.CompilerParams(vmem_limit_bytes=VMEM_LIMIT),
        name="correlate",
    )(series, series, beams.reshape(CHUNKS, FREQ * 16, 128))
    return (visibilities, beam_volts)


def solution(mesh):
    return jax.shard_map(
        body,
        mesh=mesh,
        in_specs=(P("tm", "freq", None), P(), P(), P(), P()),
        out_specs=(P(("tm", "freq"), None, None, None), P("freq", "tm", None, None)),
        check_vma=False,
    )
```

time: 75.9 us -> 61.2 us (0.81)
  Pallas kernels: 71.5 us -> 60.4 us
  local copies, waits for them, and re-layouts: 3.39 us -> 0 us
    pallas_call x1, Pallas kernels: 62.7 us -> 52.7 us  [body(): pl.pallas_call(main_kernel, out_shape=(jax.ShapeDtypeStruct((ANT, 384), b...]
    reshape x2 -> x0, local copies, waits for them, and re-layouts: 3.39 us -> none  [body(): beam_volts = beams.reshape(FREQ, 16, 2, 192).transpose(1, 0, 2, 3)]
    pallas_call x1, Pallas kernels: 8.77 us -> 7.67 us  [body(): pl.pallas_call(vis_kernel, grid=(VSTEPS,), out_shape=(jax.ShapeDtypeStruc...]
where the time goes in v2:
time: 61.2 us; the launch traced here: 61 us
  Pallas kernels  60.4 us (99%)
  between operations  0.64 us (1%)
    pallas_call x1, Pallas kernels, body(): pl.pallas_call(main_kernel, out_shape=(jax.ShapeDtypeStruct((ANT, 384), b...  52.7 us
    pallas_call x1, Pallas kernels, body(): pl.pallas_call(vis_kernel, grid=(VSTEPS,), out_shape=(jax.ShapeDtypeStruc...  7.67 us

profile of v2, /device:TPU:0, one launch (start us, length us, event | category | flops | bytes accessed | tf_op | source)
XLA Modules:
  0.0 61.0 jit_solution(4250060654690109469)
XLA Ops:
  0.6 52.7 %channelize.1 = (bf16[1024,384]{1,0:T(8,128)(2,1)}, bf16[3,32,16,128]{3,2,1,0:T(8,128)(2,1)}) custom-call(bf16[1,32,258048]{2,1,0:T(8,128)(2,1)} %v_hbm.1, f32[16,4096]{1,0:T(8,128)} %constant.2.clone.taps_hbm, s32[1,128]{1,0:T(1,128)} %bitcast.7, s32[128]{0:T(128)} %bins_smem.1, s32[1,1024]{1,0:T(1,128)} %bitcast.5, s32[1,512]{1,0:T(1,128)} %bitcast.6, ...), custom_call_target="tpu_custom_call" | custom-call | tf_op jit(solution)/shard_map/channelize/pallas_call | solution.py:332
  53.3 7.7 %correlate.1 = (f32[1,2,1024,1024]{3,2,1,0:T(8,128)}, f32[16,32,2,192]{3,2,1,0:T(2,128)}) custom-call(bf16[1024,384]{1,0:T(8,128)(2,1)} %get-tuple-element.4.series_ref.part_ref, bf16[1024,384]{1,0:T(8,128)(2,1)} %get-tuple-element.4.series_ref.part_ref, bf16[3,512,128]{2,1,0:T(8,128)(2,1)} %bitcast.4), custom_call_target="tpu_custom_call" | custom-call | tf_op jit(solution)/shard_map/correlate/pallas_call | solution.py:384

commit v3 on v2

--- a/solution.py
+++ b/solution.py
@@ -133,14 +133,17 @@
         small.wait()
     bins_col = column(bins_row[...].astype(f32)).astype(i32)
     low_cos, low_sin = turns(((bins_col * lane_iota()) & (NFFT - 1)).astype(f32) * (4.0 / NFFT))
-    high_cos, high_sin = turns(((bins_col * lane_iota()) & 31).astype(f32) * (4.0 / 32))
+    step_cos, step_sin = turns((bins_col & 31).astype(f32) * (4.0 / 32))
     scale = 1.0 / math.sqrt(NFFT)
-    low_cos, low_sin = low_cos * scale, low_sin * scale
-    for h in range(NFFT // 128):
-        hc = jnp.broadcast_to(high_cos[:, h : h + 1], (128, 128))
-        hs = jnp.broadcast_to(high_sin[:, h : h + 1], (128, 128))
-        table[0:CHAN, h * 128 : (h + 1) * 128] = (low_cos * hc - low_sin * hs).astype(bf16)
-        table[CHAN : 2 * CHAN, h * 128 : (h + 1) * 128] = (-(low_sin * hc + low_cos * hs)).astype(bf16)
+    low_cos, low_neg = low_cos * scale, low_sin * -scale
+    for cb in range(CHAN // 32):
+        rows = slice(cb * 32, (cb + 1) * 32)
+        real, imag, turn_real, turn_imag = low_cos[rows], low_neg[rows], step_cos[rows], -step_sin[rows]
+        for h in range(NFFT // 128):
+            at = slice(h * 128, (h + 1) * 128)
+            table[rows, at] = real.astype(bf16)
+            table[CHAN + cb * 32 : CHAN + (cb + 1) * 32, at] = imag.astype(bf16)
+            real, imag = real * turn_real - imag * turn_imag, real * turn_imag + imag * turn_real
 
     def filter_block(jc, nb, rb):
         c0 = pl.multiple_of(nb * 256, 256)
@@ -291,38 +294,48 @@
         pltpu.make_async_copy(stage2.at[jc], beams_hbm.at[jc], recv2_sem.at[jc]).wait()
 
 
-def vis_kernel(series_ref, part_ref, beams_ref, vis_ref, out_ref):
-    part = part_ref[...]
-    swapped = []
+def vis_kernel(series_ref, beams_hbm, vis_hbm, out_hbm, vis, beams_ref, ordered, sems, beam_sem, out_sem):
+    fetch = pltpu.make_async_copy(beams_hbm, beams_ref, beam_sem)
+    fetch.start()
+    count = ANT // VSTEPS
+    copies = []
+    for step in range(VSTEPS):
+        rows = slice(step * count, (step + 1) * count)
+        part = series_ref[rows, :]
+        swapped = []
+        for jc in range(CHUNKS):
+            chunk = part[:, jc * 128 : (jc + 1) * 128].astype(f32)
+            sign = jnp.where(lane_iota(*chunk.shape) < 64, 1.0, -1.0)
+            swapped.append((pltpu.roll(chunk, 64, 1) * sign).astype(bf16))
+        pair = jnp.concatenate([part, jnp.concatenate(swapped, 1)], 0)
+        for bb in range(4):
+            cols = slice(bb * 256, (bb + 1) * 256)
+            out = lax.dot_general(pair, series_ref[cols, :], (((1,), (1,)), ((), ())), preferred_element_type=f32)
+            out = out * (1.0 / 192.0)
+            vis[0, rows, cols] = out[:count]
+            vis[1, rows, cols] = out[count:]
+        copies.append(pltpu.make_async_copy(vis.at[:, rows, :], vis_hbm.at[0, :, rows, :], sems.at[step]))
+        copies[-1].start()
+
+    fetch.wait()
+    moves = []
     for jc in range(CHUNKS):
-        chunk = part[:, jc * 128 : (jc + 1) * 128].astype(f32)
-        sign = jnp.where(lane_iota(*chunk.shape) < 64, 1.0, -1.0)
-        swapped.append((pltpu.roll(chunk, 64, 1) * sign).astype(bf16))
-    pair = jnp.concatenate([part, jnp.concatenate(swapped, 1)], 0)
-    count = ANT // VSTEPS
-    for bb in range(4):
-        cols = slice(bb * 256, (bb + 1) * 256)
-        out = lax.dot_general(pair, series_ref[cols, :], (((1,), (1,)), ((), ())), preferred_element_type=f32)
-        out = out * (1.0 / 192.0)
-        vis_ref[0, 0, :, cols] = out[:count]
-        vis_ref[0, 1, :, cols] = out[count:]
-
-    @pl.when(pl.program_id(0) == VSTEPS // 2)
-    def _():
-        moves = []
-        for jc in range(CHUNKS):
-            rows = lax.broadcasted_iota(i32, (128, 512), 0)
-            to = (rows >> 6) * 256 + ((rows >> 4) & 3) * 48 + jc * JB + (rows & 15)
-            moves.append(jnp.where(to == lane_iota(128, 512), 1.0, 0.0).astype(bf16))
-        moves = jnp.concatenate(moves, 0)
-        for cb in range(4):
-            found = jnp.concatenate([beams_ref[jc, cb * 128 : (cb + 1) * 128, :] for jc in range(CHUNKS)], 1)
-            total = jnp.dot(found, moves, preferred_element_type=f32)
-            for u in range(8):
-                for r in range(2):
-                    rows = slice(u * 16, (u + 1) * 16)
-                    out_ref[:, cb * 8 + u, r, 0:128] = total[rows, r * 256 : r * 256 + 128]
-                    out_ref[:, cb * 8 + u, r, 128:192] = total[rows, r * 256 + 128 : r * 256 + 192]
+        row = lax.broadcasted_iota(i32, (128, 512), 0)
+        to = (row >> 6) * 256 + ((row >> 4) & 3) * 48 + jc * JB + (row & 15)
+        moves.append(jnp.where(to == lane_iota(128, 512), 1.0, 0.0).astype(bf16))
+    moves = jnp.concatenate(moves, 0)
+    for cb in range(FREQ // 8):
+        found = jnp.concatenate([beams_ref[jc, cb * 128 : (cb + 1) * 128, :] for jc in range(CHUNKS)], 1)
+        total = jnp.dot(found, moves, preferred_element_type=f32)
+        for u in range(8):
+            for r in range(2):
+                rows = slice(u * 16, (u + 1) * 16)
+                ordered[:, cb * 8 + u, r, 0:128] = total[rows, r * 256 : r * 256 + 128]
+                ordered[:, cb * 8 + u, r, 128:192] = total[rows, r * 256 + 128 : r * 256 + 192]
+    copies.append(pltpu.make_async_copy(ordered, out_hbm, out_sem))
+    copies[-1].start()
+    for copy in copies:
+        copy.wait()
 
 
 def body(voltages, chan_bins, antenna_map, beam_index, delays):
@@ -380,26 +393,25 @@
         beam_index.reshape(1, BEAMS),
         delays,
     )
-    rows = ANT // VSTEPS
     visibilities, beam_volts = pl.pallas_call(
         vis_kernel,
-        grid=(VSTEPS,),
         out_shape=(
             jax.ShapeDtypeStruct((1, 2, ANT, ANT), f32),
             jax.ShapeDtypeStruct((16, FREQ, 2, 192), f32),
         ),
-        in_specs=[
-            pl.BlockSpec(memory_space=pltpu.VMEM),
-            pl.BlockSpec((rows, 384), lambda i: (i, 0)),
-            pl.BlockSpec(memory_space=pltpu.VMEM),
+        in_specs=[pl.BlockSpec(memory_space=pltpu.VMEM), hbm],
+        out_specs=(anywhere, anywhere),
+        scratch_shapes=[
+            pltpu.VMEM((2, ANT, ANT), f32),
+            pltpu.VMEM((CHUNKS, FREQ * 16, 128), bf16),
+            pltpu.VMEM((16, FREQ, 2, 192), f32),
+            dma((VSTEPS,)),
+            dma,
+            dma,
         ],
-        out_specs=(
-            pl.BlockSpec((1, 2, rows, ANT), lambda i: (0, 0, i, 0)),
-            pl.BlockSpec((16, FREQ, 2, 192), lambda i: (0, 0, 0, 0)),
-        ),
         compiler_params=pltpu.CompilerParams(vmem_limit_bytes=VMEM_LIMIT),
         name="correlate",
-    )(series, series, beams.reshape(CHUNKS, FREQ * 16, 128))
+    )(series, beams.reshape(CHUNKS, FREQ * 16, 128))
     return (visibilities, beam_volts)
 
 

time: 61.2 us -> 58.5 us (0.956)
  Pallas kernels: 60.4 us -> 57.7 us
    pallas_call x1, Pallas kernels: 7.67 us -> 5.59 us  [body(): pl.pallas_call(vis_kernel, out_shape=(jax.ShapeDtypeStruct((1, 2, ANT, AN...]
where the time goes in v3:
time: 58.5 us; the launch traced here: 58.4 us
  Pallas kernels  57.7 us (99%)
  between operations  0.64 us (1%)
    pallas_call x1, Pallas kernels, body(): pl.pallas_call(main_kernel, out_shape=(jax.ShapeDtypeStruct((ANT, 384), b...  52.1 us
    pallas_call x1, Pallas kernels, body(): pl.pallas_call(vis_kernel, out_shape=(jax.ShapeDtypeStruct((1, 2, ANT, AN...  5.59 us

profile of v3, /device:TPU:0, one launch (start us, length us, event | category | flops | bytes accessed | tf_op | source)
XLA Modules:
  0.0 58.4 jit_solution(16757251796026607337)
XLA Ops:
  0.6 52.1 %channelize.1 = (bf16[1024,384]{1,0:T(8,128)(2,1)}, bf16[3,32,16,128]{3,2,1,0:T(8,128)(2,1)}) custom-call(bf16[1,32,258048]{2,1,0:T(8,128)(2,1)} %v_hbm.1, f32[16,4096]{1,0:T(8,128)} %constant.2.clone.taps_hbm, s32[1,128]{1,0:T(1,128)} %bitcast.7, s32[128]{0:T(128)} %bins_smem.1, s32[1,1024]{1,0:T(1,128)} %bitcast.5, s32[1,512]{1,0:T(1,128)} %bitcast.6, ...), custom_call_target="tpu_custom_call" | custom-call | tf_op jit(solution)/shard_map/channelize/pallas_call | solution.py:345
  52.8 5.6 %correlate.1 = (f32[1,2,1024,1024]{3,2,1,0:T(8,128)}, f32[16,32,2,192]{3,2,1,0:T(2,128)}) custom-call(bf16[1024,384]{1,0:T(8,128)(2,1)} %get-tuple-element.4.series_ref, bf16[3,512,128]{2,1,0:T(8,128)(2,1)} %bitcast.4), custom_call_target="tpu_custom_call" | custom-call | tf_op jit(solution)/shard_map/correlate/pallas_call | solution.py:396

commit v4 on v3

--- a/solution.py
+++ b/solution.py
@@ -24,7 +24,7 @@
 EACH = 7
 VSTEPS = 4
 VMEM_LIMIT = 60 * 1024 * 1024
-MESH = pl.DeviceIdType.MESH
+FLAT = pl.DeviceIdType.LOGICAL
 f32 = jnp.float32
 bf16 = jnp.bfloat16
 i32 = jnp.int32
@@ -74,16 +74,16 @@
 
     def peer_id(i):
         peer = (me + i) & (NDEV - 1)
-        return peer, (peer >> 5, peer & (FREQ - 1))
+        return peer, peer
 
     def greet(i):
-        pl.semaphore_signal(barrier, inc=1, device_id=peer_id(i)[1], device_id_type=MESH)
+        pl.semaphore_signal(barrier, inc=1, device_id=peer_id(i)[1], device_id_type=FLAT)
 
     def send(jc, i):
         peer, where = peer_id(i)
         pltpu.make_async_remote_copy(
             src_ref=stage.at[jc, peer], dst_ref=recv.at[jc, me], send_sem=send_sem.at[jc], recv_sem=recv_sem.at[jc],
-            device_id=where, device_id_type=MESH,
+            device_id=where, device_id_type=FLAT,
         ).start()
 
     def ahead(act):
@@ -91,8 +91,8 @@
         def _(i):
             act(i)
 
-    def beside(step, act):
-        for u in range(EACH):
+    def beside(step, act, part):
+        for u in range(part * EACH // 4, (part + 1) * EACH // 4):
             act(NDEV - 16 * EACH + step * EACH + u)
 
     first = JB + TAPS - 1
@@ -181,9 +181,10 @@
                     at = pl.ds(0, first * quarter)
                     pltpu.make_async_copy(v_hbm.at[0, :, at], vbuf.at[:, at], v_sem.at[nb // 4]).wait()
 
-            beside(nb, act)
             for rb in range(SIGD // 8):
                 filter_block(jc, nb, rb)
+            for part in range(4):
+                beside(nb, act, part)
 
         for nt in range(2):
             out = lax.dot_general(
@@ -215,12 +216,12 @@
 
     @pl.loop(0, BEAMS // 32)
     def _(pb):
-        beside(pb, functools.partial(send, 2))
         row = pl.multiple_of(pb * 32, 32)
         for part in range(4):
             cos, sin = turns(delays[pl.ds(row, 32), part * 256 : (part + 1) * 256] * bin_value)
             weights[pl.ds(row, 32), part * 256 : (part + 1) * 256] = cos.astype(bf16)
             weights[pl.ds(BEAMS + row, 32), part * 256 : (part + 1) * 256] = sin.astype(bf16)
+            beside(pb, functools.partial(send, 2), part)
 
     lanes = lane_iota()
     signal = (lanes // 4) * SIGD + lax.rem(lanes, 4) * 8
@@ -276,7 +277,7 @@
                 peer = (me_f + i) & (FREQ - 1)
                 pltpu.make_async_remote_copy(
                     src_ref=stage2.at[jc, peer], dst_ref=beams_hbm.at[jc, me_f], send_sem=send2_sem.at[jc],
-                    recv_sem=recv2_sem.at[jc], device_id=(me_tm, peer), device_id_type=MESH,
+                    recv_sem=recv2_sem.at[jc], device_id=me_tm * FREQ + peer, device_id_type=FLAT,
                 ).start()
 
     beamform(0, 2)

time: 58.5 us -> 58.3 us (level)
  no operation moved by 1% of the time
where the time goes in v4:
time: 58.3 us; the launch traced here: 58.1 us
  Pallas kernels  57.5 us (99%)
  between operations  0.64 us (1%)
    pallas_call x1, Pallas kernels, body(): pl.pallas_call(main_kernel, out_shape=(jax.ShapeDtypeStruct((ANT, 384), b...  51.9 us
    pallas_call x1, Pallas kernels, body(): pl.pallas_call(vis_kernel, out_shape=(jax.ShapeDtypeStruct((1, 2, ANT, AN...  5.58 us

profile of v4, /device:TPU:0, one launch (start us, length us, event | category | flops | bytes accessed | tf_op | source)
XLA Modules:
  0.0 58.1 jit_solution(10689519023354630775)
XLA Ops:
  0.6 51.9 %channelize.1 = (bf16[1024,384]{1,0:T(8,128)(2,1)}, bf16[3,32,16,128]{3,2,1,0:T(8,128)(2,1)}) custom-call(bf16[1,32,258048]{2,1,0:T(8,128)(2,1)} %v_hbm.1, f32[16,4096]{1,0:T(8,128)} %constant.2.clone.taps_hbm, s32[1,128]{1,0:T(1,128)} %bitcast.7, s32[128]{0:T(128)} %bins_smem.1, s32[1,1024]{1,0:T(1,128)} %bitcast.5, s32[1,512]{1,0:T(1,128)} %bitcast.6, ...), custom_call_target="tpu_custom_call" | custom-call | tf_op jit(solution)/shard_map/channelize/pallas_call | solution.py:346
  52.5 5.6 %correlate.1 = (f32[1,2,1024,1024]{3,2,1,0:T(8,128)}, f32[16,32,2,192]{3,2,1,0:T(2,128)}) custom-call(bf16[1024,384]{1,0:T(8,128)(2,1)} %get-tuple-element.4.series_ref, bf16[3,512,128]{2,1,0:T(8,128)(2,1)} %bitcast.4), custom_call_target="tpu_custom_call" | custom-call | tf_op jit(solution)/shard_map/correlate/pallas_call | solution.py:397
